TPU v7x, 128 devices: a whole 4x4x4 slice. The times are simulated.
128 devices in a mesh: blk: 32 (over x, z, y_lo), group: 4 (over y_hi, core).
Axes of the slice: x: 4, y: 4 (y_hi: 2, y_lo: 2; y = y_hi * 2 + y_lo), z: 4, core: 2. Of those that a mesh axis runs over, the one named last changes fastest.
Arguments:
- queries: bfloat16 [32, 2048, 2560], P('blk', 'group'), may hold values from -6 to 6
- new_keys: bfloat16 [32, 2048, 256], P('blk', 'group'), may hold values from -15 to 15
- new_values: bfloat16 [32, 2048, 256], P('blk', 'group'), may hold values from -4 to 4
- key_cache: bfloat16 [1280, 128, 256], P('blk', 'group'), may hold values from -4 to 4
- value_cache: bfloat16 [1280, 128, 256], P('blk', 'group'), may hold values from -4 to 4
- out_weight: bfloat16 [2560, 2560], replicated, may hold values from -0.375 to 0.375
- lengths: int32 [32], replicated, may hold values from 0 to 30720, as said below
- page_table: int32 [32, 32], replicated, may hold values from 0 to 1279, as said below
Outputs:
- hidden_states: bfloat16 [32, 2048, 2560], P('blk', 'group')
- key_cache_out: bfloat16 [1280, 128, 256], P('blk', 'group')
- value_cache_out: bfloat16 [1280, 128, 256], P('blk', 'group')
Inputs may be any that keep to these rules, and one draw needn't show every extreme that they name: `lengths`: multiples of 2048; some request has length 0 and some has 30720. `page_table`: all entries differ; page p lies on blk index p // 40; columns below 16 hold the request's last 16 pages before its group in order (pages that hold no part of a request where its length is short), the others the pages of its group in order; of one request's first 16 entries at most 1 lie on one blk index, of its last 16 at most 1, and both bounds are reached for every request.
All inputs are finite; a program needn't handle non-finite values.
Results may differ from a plain program's by a relative error of at most 0.009.
Values may be sent and summed in bfloat16 or wider, within the bound.
A program may use at most 256 MiB of HBM per device.

v0:
```python
import jax
import jax.numpy as jnp
from jax import lax
from jax.sharding import PartitionSpec as P

masked_score = -1e30
key_block_size = 512


def rotate(values, positions):
    quarter = values.shape[-1] // 4
    freq_table = 10000.0 ** (-jnp.arange(quarter, dtype=jnp.float32) / quarter)
    angles = positions.astype(jnp.float32)[..., None] * freq_table
    cosine = jnp.cos(angles)
    sine_part = jnp.sin(angles)
    leading = values[..., :quarter]
    trailing = values[..., quarter : 2 * quarter]
    return jnp.concatenate(
        [
            leading * cosine - trailing * sine_part,
            trailing * cosine + leading * sine_part,
            values[..., 2 * quarter :],
        ],
        axis=-1,
    )


def attend_block(carried, query_block, key_rows, value_rows, visible, score_scale):
    running_max, running_sum, running_acc = carried
    scores = (
        jnp.einsum("thd,kd->thk", query_block, key_rows, preferred_element_type=jnp.float32)
        * score_scale
    )
    scores = jnp.where(visible, scores, masked_score)
    new_max = jnp.maximum(running_max, jnp.max(scores, axis=2))
    weights = jnp.where(visible, jnp.exp(scores - new_max[:, :, None]), 0.0)
    factor = jnp.exp(running_max - new_max)
    new_sum = running_sum * factor + jnp.sum(weights, axis=2)
    new_acc = running_acc * factor[:, :, None] + jnp.einsum(
        "thk,kd->thd", weights.astype(jnp.bfloat16), value_rows, preferred_element_type=jnp.float32
    )
    return (new_max, new_sum, new_acc)


def attend(carried, query_block, key_rows, value_rows, visible, score_scale):
    key_total = key_rows.shape[0]
    for block_start in range(0, key_total, key_block_size):
        block_stop = min(block_start + key_block_size, key_total)
        carried = attend_block(
            carried,
            query_block,
            key_rows[block_start:block_stop],
            value_rows[block_start:block_stop],
            visible[:, :, block_start:block_stop],
            score_scale,
        )
    return carried


def body(queries, new_keys, new_values, key_cache, value_cache, out_weight, lengths, page_table):
    blk_count = lax.axis_size("blk")
    blk_index = lax.axis_index("blk")
    group_count = lax.axis_size("group")
    group_index = lax.axis_index("group")
    tok_rows = queries.shape[1]
    head_dim = new_keys.shape[2]
    head_count = queries.shape[2] // head_dim
    pages_here = key_cache.shape[0]
    page_rows = key_cache.shape[1]
    page_len = page_rows * group_count
    slot_count = page_table.shape[1]
    group_len = tok_rows * group_count
    fresh_pages = group_len // page_len
    window_pages = slot_count - fresh_pages
    window_len = window_pages * page_len
    score_scale = head_dim ** (-0.5)
    length = lengths[blk_index]
    my_table = page_table[blk_index]
    offsets = group_index * tok_rows + jnp.arange(tok_rows, dtype=jnp.int32)
    positions = length + offsets
    roped_queries = rotate(
        queries[0].astype(jnp.float32).reshape(tok_rows, head_count, head_dim), positions[:, None]
    ).astype(jnp.bfloat16)
    roped_keys = rotate(new_keys[0].astype(jnp.float32), positions).astype(jnp.bfloat16)
    all_keys, all_values = (
        lax.all_gather(roped_keys, "group", axis=0, tiled=True),
        lax.all_gather(new_values[0], "group", axis=0, tiled=True),
    )
    key_index = jnp.arange(group_len, dtype=jnp.int32)
    fresh_visible = key_index[None, :] <= offsets[:, None]
    initial = (
        jnp.full((tok_rows, head_count), masked_score, jnp.float32),
        jnp.zeros((tok_rows, head_count), jnp.float32),
        jnp.zeros((tok_rows, head_count, head_dim), jnp.float32),
    )
    carried = attend(
        initial, roped_queries, all_keys, all_values, fresh_visible[:, None, :], score_scale
    )
    old_table = my_table[:window_pages]
    blank_pages = jnp.zeros((window_pages, page_rows, head_dim), jnp.bfloat16)
    pieces = (
        lax.all_gather(key_cache, "blk", axis=0, tiled=True),
        lax.all_gather(value_cache, "blk", axis=0, tiled=True),
    )
    held_pages = pieces[0].shape[0]
    inside = (old_table >= 0) & (old_table < held_pages)
    clipped = jnp.clip(old_table, 0, held_pages - 1)
    old_keys = jnp.where(inside[:, None, None], pieces[0][clipped], blank_pages)
    old_values = jnp.where(inside[:, None, None], pieces[1][clipped], blank_pages)
    pieces = (
        lax.all_gather(old_keys, "group", axis=1, tiled=True),
        lax.all_gather(old_values, "group", axis=1, tiled=True),
    )
    piece_rows = pieces[0].shape[1]
    key_rows = pieces[0].reshape(-1, head_dim)
    value_rows = pieces[1].reshape(-1, head_dim)
    in_window = (
        jnp.arange(window_pages, dtype=jnp.int32)[:, None] * page_len
        + jnp.arange(piece_rows, dtype=jnp.int32)[None, :]
    ).reshape(-1)
    visible = (in_window[None, :] > offsets[:, None]) & (
        length - window_len + in_window[None, :] >= 0
    )
    carried = attend(carried, roped_queries, key_rows, value_rows, visible[:, None, :], score_scale)
    running_max, running_sum, running_acc = carried
    attended = (
        (running_acc / running_sum[:, :, None])
        .astype(jnp.bfloat16)
        .reshape(tok_rows, head_count * head_dim)
    )
    hidden = jnp.dot(attended, out_weight, preferred_element_type=jnp.float32).astype(jnp.bfloat16)[
        None
    ]
    cap_new = (fresh_pages + blk_count - 1) // blk_count
    quarter_keys = lax.dynamic_index_in_dim(
        all_keys.reshape(fresh_pages, group_count, page_rows, head_dim),
        group_index,
        axis=1,
        keepdims=False,
    )
    quarter_values = lax.dynamic_index_in_dim(
        all_values.reshape(fresh_pages, group_count, page_rows, head_dim),
        group_index,
        axis=1,
        keepdims=False,
    )
    new_owner = my_table[window_pages:] // pages_here
    fresh_ids = jnp.arange(fresh_pages, dtype=jnp.int32)
    before = fresh_ids[None, :] < fresh_ids[:, None]
    new_rank = jnp.sum(
        (before & (new_owner[None, :] == new_owner[:, None])).astype(jnp.int32), axis=1
    )
    placing = (
        (new_owner[None, None, :] == jnp.arange(blk_count, dtype=jnp.int32)[:, None, None])
        & (new_rank[None, None, :] == jnp.arange(cap_new, dtype=jnp.int32)[None, :, None])
    ).astype(jnp.bfloat16)
    send_new_keys = jnp.einsum(
        "ocj,jrd->ocrd", placing, quarter_keys, preferred_element_type=jnp.float32
    ).astype(jnp.bfloat16)
    send_new_values = jnp.einsum(
        "ocj,jrd->ocrd", placing, quarter_values, preferred_element_type=jnp.float32
    ).astype(jnp.bfloat16)
    arrived_keys, arrived_values = (
        lax.all_to_all(send_new_keys, "blk", split_axis=0, concat_axis=0, tiled=True),
        lax.all_to_all(send_new_values, "blk", split_axis=0, concat_axis=0, tiled=True),
    )
    owned_slots = page_table[:, window_pages:] // pages_here == blk_index
    hit_rank = jnp.cumsum(owned_slots.astype(jnp.int32), axis=1) - 1
    choose = owned_slots[:, None, :] & (
        hit_rank[:, None, :] == jnp.arange(cap_new, dtype=jnp.int32)[None, :, None]
    )
    target = jnp.where(
        jnp.any(choose, axis=2),
        jnp.sum(jnp.where(choose, page_table[:, None, window_pages:] % pages_here, 0), axis=2),
        pages_here,
    )
    key_out = key_cache.at[target.reshape(-1)].set(
        arrived_keys.reshape(-1, page_rows, head_dim), mode="drop"
    )
    value_out = value_cache.at[target.reshape(-1)].set(
        arrived_values.reshape(-1, page_rows, head_dim), mode="drop"
    )
    return (hidden, key_out, value_out)


def solution(mesh):
    return jax.shard_map(
        body,
        mesh=mesh,
        in_specs=(
            P("blk", "group", None),
            P("blk", "group", None),
            P("blk", "group", None),
            P("blk", "group", None),
            P("blk", "group", None),
            P(),
            P(),
            P(),
        ),
        out_specs=(P("blk", "group", None), P("blk", "group", None), P("blk", "group", None)),
        check_vma=False,
    )
```

profile of v0, /device:TPU:0, one launch (start us, length us, event | category | flops | bytes accessed | tf_op | source)
XLA Modules:
  0.0 1177.1 jit_solution(8598591531830800221)
XLA Ops:
  20.2 4.4 copy.70
  33.3 3.5 subtract_convert_fusion
  46.5 9.4 all-to-all-start
  56.2 11.0 all-gather.18.cloned.1.call-done
  72.0 7.3 fusion.3
  79.3 437.6 %all-gather.10.cloned.1.call-done = bf16[1280,32,256]{2,1,0:T(8,128)(2,1)} async-done(((bf16[40,32,256]{2,1,0:T(8,128)(2,1)}), bf16[1280,32,256]{2,1,0:T(8,128)(2,1)}) %all-gather.10.cloned.1.call-update) | async-done | bytes 20971536 | tf_op jit(solution)/shard_map/all_gather | solution.py:102
  517.0 7.5 gather_fusion
  524.5 443.7 %all-gather.14.cloned.1.call-done = bf16[1280,32,256]{2,1,0:T(8,128)(2,1)} async-done(((bf16[40,32,256]{2,1,0:T(8,128)(2,1)}), bf16[1280,32,256]{2,1,0:T(8,128)(2,1)}) %all-gather.14.cloned.1.call-update) | async-done | bytes 20971536 | tf_op jit(solution)/shard_map/all_gather | solution.py:103
  968.2 7.5 gather_fusion.1
  976.7 7.5 fusion.2
  984.2 7.3 fusion.1
  991.5 10.9 all-to-all-start.1
  1002.4 7.4 fusion
  1009.9 3.4 scatter_fusion
  1017.9 7.4 fusion.4
  1025.4 5.8 fusion.5
  1031.2 5.8 fusion.6
  1039.7 3.1 copy-done
  1042.8 3.1 fusion.22
  1047.2 10.0 fusion.24
  1057.2 7.1 fusion.20
  1064.3 9.8 fusion.26
  1077.2 10.1 fusion.28
  1087.3 3.1 fusion.16
  1090.4 9.8 fusion.30
  1106.5 7.6 fusion.12
  1114.2 3.1 fusion.10
  1119.0 5.6 fusion.32
  1124.6 9.5 fusion.34
  1134.2 4.7 fusion.36
  1138.9 19.2 %divide_convert_fusion = bf16[512,10,256]{0,2,1:T(8,128)(2,1)} fusion(f32[512,10,256]{0,2,1:T(8,128)} %fusion.24, f32[512,10,256]{0,2,1:T(8,128)} %fusion.26, f32[512,10,256]{0,2,1:T(8,128)} %fusion.28, f32[512,10,256]{0,2,1:T(8,128)} %fusion.30, f32[512,10,256]{0,2,1:T(8,128)} %fusion.32, f32[512,10,256]{0,2,1:T(8,128)} %fusion.34, ...), kind=kOutput, calls=%fused_computation.52 | convolution fusion | flops 1377566720 | bytes 50536448 | tf_op jit(solution)/shard_map/thk,kd->thd/dot_general | solution.py:39
  1158.1 12.0 %fusion.80 = bf16[1,512,2560]{2,1,0:T(8,128)(2,1)} fusion(bf16[512,2560]{0,1:T(8,128)(2,1)} %bitcast.170, bf16[2560,2560]{1,0:T(8,128)(2,1)} %param.13), kind=kOutput, calls=%fused_computation.96 | convolution fusion | flops 6712197120 | bytes 18350080 | tf_op jit(solution)/shard_map/dot_general | solution.py:131
  (161 shorter events, 56.3 us)
Async XLA Ops:
  7.2 36.8 %all-gather.8.cloned.1.call-start = ((), (), s32[]{:S(2)}) async-start(), calls=%async_computation.2 | async-start | bytes 1310720 | tf_op jit(solution)/shard_map/all_gather | solution.py:86
  17.0 50.3 %all-gather.18.cloned.1.call-start = ((), (), s32[]{:S(2)}) async-start(), calls=%async_computation.7 | async-start | bytes 1310720 | tf_op jit(solution)/shard_map/all_gather | solution.py:87
  18.9 498.1 %all-gather.10.cloned.1.call-start = ((), (), s32[]{:S(2)}) async-start(), calls=%async_computation.3 | async-start | bytes 21626880 | tf_op jit(solution)/shard_map/all_gather | solution.py:102
  19.6 948.6 %all-gather.14.cloned.1.call-start = ((), (), s32[]{:S(2)}) async-start(), calls=%async_computation.5 | async-start | bytes 21626880 | tf_op jit(solution)/shard_map/all_gather | solution.py:103
  39.3 944.9 %copy-start.5 = (bf16[512,10,256]{2,0,1:T(8,128)(2,1)}, bf16[512,10,256]{2,0,1:T(8,128)(2,1)S(1)}, u32[]{:S(2)}) copy-start(bf16[512,10,256]{2,0,1:T(8,128)(2,1)S(1)} %pad_maximum_fusion) | copy-start | bytes 7864324
  42.8 36.5 %copy-start.11 = (pred[512,512]{0,1:T(8,128)(4,1)}, pred[512,512]{0,1:T(8,128)(4,1)S(1)}, u32[]{:S(2)}) copy-start(pred[512,512]{0,1:T(8,128)(4,1)S(1)} %get-tuple-element.31) | copy-start | bytes 786436
  46.5 945.1 %all-to-all-start = ((bf16[32,1,32,256]{3,2,1,0:T(8,128)(2,1)}), bf16[32,1,32,256]{3,2,1,0:T(8,128)(2,1)}, u32[]{:S(2)}, u32[]{:S(2)}) async-start(bf16[32,1,32,256]{3,2,1,0:T(8,128)(2,1)} %copy.87), calls=%async_computation | async-start | bytes 1048576 | tf_op jit(solution)/shard_map/all_to_all | solution.py:164
  55.9 960.5 %all-gather.12.cloned.1.call-start = ((), (), s32[]{:S(2)}) async-start(), calls=%async_computation.4 | async-start | bytes 1310720 | tf_op jit(solution)/shard_map/all_gather | solution.py:111
  991.5 18.4 %copy-start.3 = (bf16[40,32,256]{2,1,0:T(8,128)(2,1)S(1)}, bf16[40,32,256]{2,1,0:T(8,128)(2,1)}, u32[]{:S(2)}) copy-start(bf16[40,32,256]{2,1,0:T(8,128)(2,1)} %copy.115) | copy-start | bytes 1966084
  991.5 22.7 %copy-start.1 = (bf16[40,32,256]{2,1,0:T(8,128)(2,1)S(1)}, bf16[40,32,256]{2,1,0:T(8,128)(2,1)}, u32[]{:S(2)}) copy-start(bf16[40,32,256]{2,1,0:T(8,128)(2,1)} %copy.116) | copy-start | bytes 1966084
  991.5 22.7 %all-to-all-start.1 = ((bf16[32,1,32,256]{3,2,1,0:T(8,128)(2,1)}), bf16[32,1,32,256]{3,2,1,0:T(8,128)(2,1)S(1)}, u32[]{:S(2)}, u32[]{:S(2)}) async-start(bf16[32,1,32,256]{3,2,1,0:T(8,128)(2,1)} %copy.90), calls=%async_computation.1 | async-start | bytes 1048576 | tf_op jit(solution)/shard_map/all_to_all | solution.py:165
  1002.4 15.6 %copy-start.13 = (pred[512,512]{0,1:T(8,128)(4,1)S(1)}, pred[512,512]{0,1:T(8,128)(4,1)}, u32[]{:S(2)}) copy-start(pred[512,512]{0,1:T(8,128)(4,1)} %get-tuple-element.34) | copy-start | bytes 786436
  1002.4 43.6 %all-gather.16.cloned.1.call-start = ((), (), s32[]{:S(2)}) async-start(), calls=%async_computation.6 | async-start | bytes 1310720 | tf_op jit(solution)/shard_map/all_gather | solution.py:112
  1009.9 29.0 %copy-start.25 = (f32[512,10]{0,1:T(8,128)}, f32[512,10]{0,1:T(8,128)S(1)}, u32[]{:S(2)}) copy-start(f32[512,10]{0,1:T(8,128)S(1)} %get-tuple-element.66) | copy-start | bytes 61444
  1009.9 15.5 %copy-start.15 = (pred[512,512]{0,1:T(8,128)(4,1)S(1)}, pred[512,512]{0,1:T(8,128)(4,1)}, u32[]{:S(2)}) copy-start(pred[512,512]{0,1:T(8,128)(4,1)} %get-tuple-element.37) | copy-start | bytes 786436
  1013.3 17.9 %copy-start.4 = (bf16[40,32,256]{2,1,0:T(8,128)(2,1)}, bf16[40,32,256]{2,1,0:T(8,128)(2,1)S(1)}, u32[]{:S(2)}) copy-start(bf16[40,32,256]{2,1,0:T(8,128)(2,1)S(1)} %scatter_fusion) | copy-start | bytes 1966084
  1016.4 14.8 %copy-start.2 = (bf16[40,32,256]{2,1,0:T(8,128)(2,1)}, bf16[40,32,256]{2,1,0:T(8,128)(2,1)S(1)}, u32[]{:S(2)}) copy-start(bf16[40,32,256]{2,1,0:T(8,128)(2,1)S(1)} %scatter_fusion.1) | copy-start | bytes 1966084
  1039.7 17.6 %copy-start.20 = (f32[512,10]{0,1:T(8,128)}, f32[512,10]{0,1:T(8,128)S(1)}, u32[]{:S(2)}) copy-start(f32[512,10]{0,1:T(8,128)S(1)} %get-tuple-element.17) | copy-start | bytes 61444
  1039.7 24.6 %copy-start.21 = (f32[512,10]{0,1:T(8,128)}, f32[512,10]{0,1:T(8,128)S(1)}, u32[]{:S(2)}) copy-start(f32[512,10]{0,1:T(8,128)S(1)} %get-tuple-element.18) | copy-start | bytes 61444
  1039.7 37.5 %copy-start.22 = (f32[512,10]{0,1:T(8,128)}, f32[512,10]{0,1:T(8,128)S(1)}, u32[]{:S(2)}) copy-start(f32[512,10]{0,1:T(8,128)S(1)} %get-tuple-element.19) | copy-start | bytes 61444
  1039.7 50.7 %copy-start.23 = (f32[512,10]{0,1:T(8,128)}, f32[512,10]{0,1:T(8,128)S(1)}, u32[]{:S(2)}) copy-start(f32[512,10]{0,1:T(8,128)S(1)} %get-tuple-element.20) | copy-start | bytes 61444
  1039.7 60.6 %copy-start.24 = (f32[512,10]{0,1:T(8,128)}, f32[512,10]{0,1:T(8,128)S(1)}, u32[]{:S(2)}) copy-start(f32[512,10]{0,1:T(8,128)S(1)} %get-tuple-element.45) | copy-start | bytes 61444
  1039.7 63.7 %copy-start.19 = (f32[512,10]{0,1:T(8,128)}, f32[512,10]{0,1:T(8,128)S(1)}, u32[]{:S(2)}) copy-start(f32[512,10]{0,1:T(8,128)S(1)} %get-tuple-element.21) | copy-start | bytes 61444
  1047.2 26.9 %slice-start.12 = ((s8[10485760]{0:T(1024)(128)(4,1)}), s8[4194304]{0:T(1024)(128)(4,1)S(1)}, s32[]{:S(2)}) async-start(s8[10485760]{0:T(1024)(128)(4,1)} %bitcast.155), calls=%async_computation.20 | async-start | bytes 8388608
  1047.2 26.9 %slice-start.13 = ((s8[10485760]{0:T(1024)(128)(4,1)}), s8[4194304]{0:T(1024)(128)(4,1)S(1)}, s32[]{:S(2)}) async-start(s8[10485760]{0:T(1024)(128)(4,1)} %bitcast.155), calls=%async_computation.21 | async-start | bytes 8388608
  1064.3 23.0 %slice-start.9 = ((s8[10485760]{0:T(1024)(128)(4,1)}), s8[4194304]{0:T(1024)(128)(4,1)S(1)}, s32[]{:S(2)}) async-start(s8[10485760]{0:T(1024)(128)(4,1)} %bitcast.153), calls=%async_computation.17 | async-start | bytes 8388608
  1064.3 23.0 %slice-start.10 = ((s8[10485760]{0:T(1024)(128)(4,1)}), s8[4194304]{0:T(1024)(128)(4,1)S(1)}, s32[]{:S(2)}) async-start(s8[10485760]{0:T(1024)(128)(4,1)} %bitcast.153), calls=%async_computation.18 | async-start | bytes 8388608
  1077.2 23.0 %slice-start.6 = ((s8[10485760]{0:T(1024)(128)(4,1)}), s8[4194304]{0:T(1024)(128)(4,1)S(1)}, s32[]{:S(2)}) async-start(s8[10485760]{0:T(1024)(128)(4,1)} %bitcast.151), calls=%async_computation.14 | async-start | bytes 8388608
  1077.2 23.0 %slice-start.7 = ((s8[10485760]{0:T(1024)(128)(4,1)}), s8[4194304]{0:T(1024)(128)(4,1)S(1)}, s32[]{:S(2)}) async-start(s8[10485760]{0:T(1024)(128)(4,1)} %bitcast.151), calls=%async_computation.15 | async-start | bytes 8388608
  1090.4 12.9 %slice-start = ((s8[10485760]{0:T(1024)(128)(4,1)}), s8[4194304]{0:T(1024)(128)(4,1)S(1)}, s32[]{:S(2)}) async-start(s8[10485760]{0:T(1024)(128)(4,1)} %bitcast.147), calls=%async_computation.8 | async-start | bytes 8388608
  1090.4 12.9 %slice-start.1 = ((s8[10485760]{0:T(1024)(128)(4,1)}), s8[4194304]{0:T(1024)(128)(4,1)S(1)}, s32[]{:S(2)}) async-start(s8[10485760]{0:T(1024)(128)(4,1)} %bitcast.147), calls=%async_computation.9 | async-start | bytes 8388608
  1090.4 12.9 %slice-start.2 = ((s8[10485760]{0:T(1024)(128)(4,1)}), s8[2097152]{0:T(1024)(128)(4,1)S(1)}, s32[]{:S(2)}) async-start(s8[10485760]{0:T(1024)(128)(4,1)} %bitcast.147), calls=%async_computation.10 | async-start | bytes 4194304
  (21 other events, 149.6 us)
Sparse Core Ops, SparseCore 0:
  17.1 23.2 all-gather.7
  42.1 25.1 all-gather.17
  69.5 447.4 all-gather.9
  518.5 449.7 all-gather.13
  976.8 23.0 all-gather.11
  1016.5 19.6 all-gather.15
where the time goes:
time: 1180 us
  waiting for transfers between devices  895 us (76%)
  matrix products  142 us (12%)
  other arithmetic  52.3 us (4%)
  local copies, waits for them, and re-layouts  51.9 us (4%)
  starting transfers between devices  20.8 us (2%)
  between operations  15.4 us (1%)
    all_gather x1, waiting for transfers between devices, body(): lax.all_gather(value_cache, 'blk', axis=0, tiled=True)  444 us
    all_gather x1, waiting for transfers between devices, body(): lax.all_gather(key_cache, 'blk', axis=0, tiled=True)  438 us
    dot_general x8, matrix products, attend_block(): jnp.einsum('thk,kd->thd', weights.astype(jnp.bfloat16), value_rows, prefe...  78.7 us
    dot_general x8, matrix products, attend_block(): jnp.einsum('thd,kd->thk', query_block, key_rows, preferred_element_type=j...  50.4 us
    reduce_sum x8, other arithmetic, attend_block(): new_sum = running_sum * factor + jnp.sum(weights, axis=2)  33.2 us
  transfers between devices with their start and end apart: 8, of which 4 were waited for; matrix products, arithmetic and copies ran while one was open for 9% of the time, Pallas kernels for 0%

commit v1 on v0

--- a/solution.py
+++ b/solution.py
@@ -99,7 +99,9 @@
     old_table = my_table[:window_pages]
     blank_pages = jnp.zeros((window_pages, page_rows, head_dim), jnp.bfloat16)
     pieces = (
-        lax.all_gather(key_cache, "blk", axis=0, tiled=True),
+        jnp.concatenate(
+            lax.all_to_all(jnp.stack([key_cache] * lax.axis_size("blk")), "blk", 0, 0), axis=0
+        ),
         lax.all_gather(value_cache, "blk", axis=0, tiled=True),
     )
     held_pages = pieces[0].shape[0]

time: 1180 us -> 988 us (0.84)
  waiting for transfers between devices: 895 us -> 685 us
    all_gather x1 -> x0, waiting for transfers between devices: 438 us -> none  [body(): lax.all_gather(key_cache, 'blk', axis=0, tiled=True)]
    all_to_all x0 -> x1, waiting for transfers between devices: none -> 315 us  [body(): lax.all_to_all(jnp.stack([key_cache] * lax.axis_size('blk')), 'blk', 0, 0)]
    all_gather x1, waiting for transfers between devices: 444 us -> 335 us  [body(): lax.all_gather(value_cache, 'blk', axis=0, tiled=True)]
    all_gather x1, waiting for transfers between devices: 11 us -> 33.1 us  [body(): lax.all_gather(new_values[0], 'group', axis=0, tiled=True)]
  transfers between devices with their start and end apart: 8 -> 8, of which waited for: 4 -> 4; matrix products, arithmetic and copies ran while one was open for 9% -> 12% of each run, Pallas kernels for 0% -> 0%
where the time goes in v1:
time: 988 us; the launch traced here: 980 us
  waiting for transfers between devices  685 us (69%)
  matrix products  138 us (14%)
  other arithmetic  56.7 us (6%)
  local copies, waits for them, and re-layouts  54 us (5%)
  starting transfers between devices  30.6 us (3%)
  between operations  15.2 us (2%)
    all_gather x1, waiting for transfers between devices, body(): lax.all_gather(value_cache, 'blk', axis=0, tiled=True)  335 us
    all_to_all x1, waiting for transfers between devices, body(): lax.all_to_all(jnp.stack([key_cache] * lax.axis_size('blk')), 'blk', 0, 0)  315 us
    dot_general x8, matrix products, attend_block(): jnp.einsum('thk,kd->thd', weights.astype(jnp.bfloat16), value_rows, prefe...  73.8 us
    dot_general x8, matrix products, attend_block(): jnp.einsum('thd,kd->thk', query_block, key_rows, preferred_element_type=j...  51.2 us
    all_gather x1, waiting for transfers between devices, body(): lax.all_gather(new_values[0], 'group', axis=0, tiled=True)  33.1 us
    reduce_sum x8, other arithmetic, attend_block(): new_sum = running_sum * factor + jnp.sum(weights, axis=2)  33 us
  transfers between devices with their start and end apart: 8, of which 4 were waited for; matrix products, arithmetic and copies ran while one was open for 12% of the time, Pallas kernels for 0%

profile of v1, /device:TPU:0, one launch (start us, length us, event | category | flops | bytes accessed | tf_op | source)
XLA Modules:
  0.0 979.6 jit_solution(4560461428958498633)
XLA Ops:
  20.0 7.4 stack.2
  27.4 9.7 all-to-all-start
  49.5 3.7 subtract_convert_fusion
  64.0 33.1 %all-gather.15.cloned.1.call-done = bf16[1,2048,256]{1,2,0:T(8,128)(2,1)} async-done(((bf16[1,512,256]{1,2,0:T(8,128)(2,1)}), bf16[1,2048,256]{1,2,0:T(8,128)(2,1)}) %all-gather.15.cloned.1.call-update) | async-done | bytes 1048592 | tf_op jit(solution)/shard_map/all_gather | solution.py:87
  101.9 7.3 fusion.3
  109.2 315.3 %all-to-all-done = bf16[32,40,32,256]{3,2,1,0:T(8,128)(2,1)} async-done(((bf16[32,40,32,256]{3,2,1,0:T(8,128)(2,1)}), bf16[32,40,32,256]{3,2,1,0:T(8,128)(2,1)}, u32[]{:S(2)}, u32[]{:S(2)}) %all-to-all-start) | async-done | bytes 20971552 | tf_op jit(solution)/shard_map/all_to_all | solution.py:103
  424.5 16.3 %all-to-all-start.1 = ((bf16[32,1,32,256]{3,2,1,0:T(8,128)(2,1)}), bf16[32,1,32,256]{3,2,1,0:T(8,128)(2,1)}, u32[]{:S(2)}, u32[]{:S(2)}) async-start(bf16[32,1,32,256]{3,2,1,0:T(8,128)(2,1)} %copy.87), calls=%async_computation.1 | async-start | bytes 1048576 | tf_op jit(solution)/shard_map/all_to_all | solution.py:166
  441.3 7.5 gather_fusion
  448.8 335.2 %all-gather.11.cloned.1.call-done = bf16[1280,32,256]{2,1,0:T(8,128)(2,1)} async-done(((bf16[40,32,256]{2,1,0:T(8,128)(2,1)}), bf16[1280,32,256]{2,1,0:T(8,128)(2,1)}) %all-gather.11.cloned.1.call-update) | async-done | bytes 20971536 | tf_op jit(solution)/shard_map/all_gather | solution.py:105
  784.0 8.2 gather_fusion.1
  794.1 7.5 fusion.2
  801.6 7.3 fusion.1
  808.9 4.0 all-to-all-start.2
  813.0 7.4 fusion
  820.5 3.4 scatter_fusion
  828.2 3.7 fusion.7
  831.9 6.3 fusion.4
  838.2 5.9 fusion.6
  844.1 5.9 fusion.5
  855.2 10.3 %fusion.24 = f32[512,10,256]{0,2,1:T(8,128)} fusion(bf16[512,256,1]{1,0,2:T(8,128)(2,1)S(1)} %bitcast.169, f32[512,10,512]{0,2,1:T(8,128)} %copy-done, f32[512,10]{0,1:T(8,128)S(1)} %get-tuple-element.17, pred[512,512]{0,1:T(8,128)(4,1)S(1)} %copy-done.18), kind=kOutput, calls=%fused_computation.44 | convolution fusion | flops 1355284480 | bytes 16273408 | tf_op jit(solution)/shard_map/thk,kd->thd/dot_general | solution.py:39
  868.6 4.7 fusion.26
  873.2 7.1 fusion.18
  880.3 9.8 %fusion.28 = f32[512,10,256]{0,2,1:T(8,128)} fusion(bf16[512,256,1]{1,0,2:T(8,128)(2,1)S(1)} %bitcast.164, f32[512,10,512]{0,2,1:T(8,128)} %get-tuple-element.57, f32[512,10]{0,1:T(8,128)S(1)} %get-tuple-element.19, pred[512,512]{0,1:T(8,128)(4,1)S(1)} %copy-done.16), kind=kOutput, calls=%fused_computation.46 | convolution fusion | flops 1355284480 | bytes 16273408 | tf_op jit(solution)/shard_map/thk,kd->thd/dot_general | solution.py:39
  893.3 9.9 %fusion.30 = f32[512,10,256]{0,2,1:T(8,128)} fusion(bf16[512,256,1]{1,0,2:T(8,128)(2,1)S(1)} %bitcast.162, f32[512,10,512]{0,2,1:T(8,128)} %get-tuple-element.59, f32[512,10]{0,1:T(8,128)S(1)} %get-tuple-element.20, pred[512,512]{0,1:T(8,128)(4,1)S(1)} %copy-done.15), kind=kOutput, calls=%fused_computation.47 | convolution fusion | flops 1355284480 | bytes 16273408 | tf_op jit(solution)/shard_map/thk,kd->thd/dot_general | solution.py:39
  903.2 3.3 fusion.8
  906.5 3.1 fusion.14
  909.6 7.2 fusion.12
  921.7 5.9 fusion.32
  927.6 9.6 fusion.34
  937.2 4.7 fusion.36
  941.9 19.0 %divide_convert_fusion = bf16[512,10,256]{0,2,1:T(8,128)(2,1)} fusion(f32[512,10,256]{0,2,1:T(8,128)} %fusion.24, f32[512,10,256]{0,2,1:T(8,128)} %fusion.26, f32[512,10,256]{0,2,1:T(8,128)} %fusion.28, f32[512,10,256]{0,2,1:T(8,128)} %fusion.30, f32[512,10,256]{0,2,1:T(8,128)} %fusion.32, f32[512,10,256]{0,2,1:T(8,128)} %fusion.34, ...), kind=kOutput, calls=%fused_computation.52 | convolution fusion | flops 1377566720 | bytes 50536448 | tf_op jit(solution)/shard_map/thk,kd->thd/dot_general | solution.py:39
  960.9 12.0 %fusion.80 = bf16[1,512,2560]{2,1,0:T(8,128)(2,1)} fusion(bf16[512,2560]{0,1:T(8,128)(2,1)} %bitcast.171, bf16[2560,2560]{1,0:T(8,128)(2,1)} %param.13), kind=kOutput, calls=%fused_computation.96 | convolution fusion | flops 6712197120 | bytes 18350080 | tf_op jit(solution)/shard_map/dot_general | solution.py:133
  (167 shorter events, 63.1 us)
Async XLA Ops:
  7.2 54.4 %all-gather.7.cloned.1.call-start = ((), (), s32[]{:S(2)}) async-start(), calls=%async_computation.3 | async-start | bytes 1310720 | tf_op jit(solution)/shard_map/all_gather | solution.py:86
  17.4 79.7 %all-gather.15.cloned.1.call-start = ((), (), s32[]{:S(2)}) async-start(), calls=%async_computation.7 | async-start | bytes 1310720 | tf_op jit(solution)/shard_map/all_gather | solution.py:87
  19.3 764.7 %all-gather.11.cloned.1.call-start = ((), (), s32[]{:S(2)}) async-start(), calls=%async_computation.5 | async-start | bytes 21626880 | tf_op jit(solution)/shard_map/all_gather | solution.py:105
  27.4 397.1 %all-to-all-start = ((bf16[32,40,32,256]{3,2,1,0:T(8,128)(2,1)}), bf16[32,40,32,256]{3,2,1,0:T(8,128)(2,1)}, u32[]{:S(2)}, u32[]{:S(2)}) async-start(bf16[32,40,32,256]{3,2,1,0:T(8,128)(2,1)} %stack.2), calls=%async_computation | async-start | bytes 41943040 | tf_op jit(solution)/shard_map/all_to_all | solution.py:103
  55.7 745.9 %copy-start.4 = (bf16[512,10,256]{2,0,1:T(8,128)(2,1)}, bf16[512,10,256]{2,0,1:T(8,128)(2,1)S(1)}, u32[]{:S(2)}) copy-start(bf16[512,10,256]{2,0,1:T(8,128)(2,1)S(1)} %pad_maximum_fusion) | copy-start | bytes 7864324
  60.4 48.8 %copy-start.12 = (pred[512,512]{0,1:T(8,128)(4,1)}, pred[512,512]{0,1:T(8,128)(4,1)S(1)}, u32[]{:S(2)}) copy-start(pred[512,512]{0,1:T(8,128)(4,1)S(1)} %get-tuple-element.31) | copy-start | bytes 786436
  424.5 384.5 %all-to-all-start.1 = ((bf16[32,1,32,256]{3,2,1,0:T(8,128)(2,1)}), bf16[32,1,32,256]{3,2,1,0:T(8,128)(2,1)}, u32[]{:S(2)}, u32[]{:S(2)}) async-start(bf16[32,1,32,256]{3,2,1,0:T(8,128)(2,1)} %copy.87), calls=%async_computation.1 | async-start | bytes 1048576 | tf_op jit(solution)/shard_map/all_to_all | solution.py:166
  440.8 385.9 %all-gather.9.cloned.1.call-start = ((), (), s32[]{:S(2)}) async-start(), calls=%async_computation.4 | async-start | bytes 1310720 | tf_op jit(solution)/shard_map/all_gather | solution.py:113
  808.9 16.0 %copy-start.1 = (bf16[40,32,256]{2,1,0:T(8,128)(2,1)S(1)}, bf16[40,32,256]{2,1,0:T(8,128)(2,1)}, u32[]{:S(2)}) copy-start(bf16[40,32,256]{2,1,0:T(8,128)(2,1)} %copy.116) | copy-start | bytes 1966084
  808.9 16.0 %all-to-all-start.2 = ((bf16[32,1,32,256]{3,2,1,0:T(8,128)(2,1)}), bf16[32,1,32,256]{3,2,1,0:T(8,128)(2,1)S(1)}, u32[]{:S(2)}, u32[]{:S(2)}) async-start(bf16[32,1,32,256]{3,2,1,0:T(8,128)(2,1)} %copy.90), calls=%async_computation.2 | async-start | bytes 1048576 | tf_op jit(solution)/shard_map/all_to_all | solution.py:167
  813.0 15.3 %copy-start.18 = (pred[512,512]{0,1:T(8,128)(4,1)S(1)}, pred[512,512]{0,1:T(8,128)(4,1)}, u32[]{:S(2)}) copy-start(pred[512,512]{0,1:T(8,128)(4,1)} %get-tuple-element.35) | copy-start | bytes 786436
  813.0 40.8 %all-gather.13.cloned.1.call-start = ((), (), s32[]{:S(2)}) async-start(), calls=%async_computation.6 | async-start | bytes 1310720 | tf_op jit(solution)/shard_map/all_gather | solution.py:114
  820.5 29.5 %copy-start.26 = (f32[512,10]{0,1:T(8,128)}, f32[512,10]{0,1:T(8,128)S(1)}, u32[]{:S(2)}) copy-start(f32[512,10]{0,1:T(8,128)S(1)} %get-tuple-element.66) | copy-start | bytes 61444
  820.5 11.4 %copy-start.14 = (pred[512,512]{0,1:T(8,128)(4,1)S(1)}, pred[512,512]{0,1:T(8,128)(4,1)}, u32[]{:S(2)}) copy-start(pred[512,512]{0,1:T(8,128)(4,1)} %get-tuple-element.34) | copy-start | bytes 786436
  823.9 14.3 %copy-start.3 = (bf16[40,32,256]{2,1,0:T(8,128)(2,1)}, bf16[40,32,256]{2,1,0:T(8,128)(2,1)S(1)}, u32[]{:S(2)}) copy-start(bf16[40,32,256]{2,1,0:T(8,128)(2,1)S(1)} %scatter_fusion) | copy-start | bytes 1966084
  826.6 11.5 %copy-start.2 = (bf16[40,32,256]{2,1,0:T(8,128)(2,1)}, bf16[40,32,256]{2,1,0:T(8,128)(2,1)S(1)}, u32[]{:S(2)}) copy-start(bf16[40,32,256]{2,1,0:T(8,128)(2,1)S(1)} %scatter_fusion.1) | copy-start | bytes 1966084
  831.9 18.7 %copy-start = (f32[512,10,512]{0,2,1:T(8,128)}, f32[512,10,512]{0,2,1:T(8,128)S(1)}, u32[]{:S(2)}) copy-start(f32[512,10,512]{0,2,1:T(8,128)S(1)} %get-tuple-element.53) | copy-start | bytes 31457284
  850.6 14.8 %copy-start.21 = (f32[512,10]{0,1:T(8,128)}, f32[512,10]{0,1:T(8,128)S(1)}, u32[]{:S(2)}) copy-start(f32[512,10]{0,1:T(8,128)S(1)} %get-tuple-element.17) | copy-start | bytes 61444
  850.6 18.0 %copy-start.22 = (f32[512,10]{0,1:T(8,128)}, f32[512,10]{0,1:T(8,128)S(1)}, u32[]{:S(2)}) copy-start(f32[512,10]{0,1:T(8,128)S(1)} %get-tuple-element.18) | copy-start | bytes 61444
  850.6 29.7 %copy-start.23 = (f32[512,10]{0,1:T(8,128)}, f32[512,10]{0,1:T(8,128)S(1)}, u32[]{:S(2)}) copy-start(f32[512,10]{0,1:T(8,128)S(1)} %get-tuple-element.19) | copy-start | bytes 61444
  850.6 42.7 %copy-start.24 = (f32[512,10]{0,1:T(8,128)}, f32[512,10]{0,1:T(8,128)S(1)}, u32[]{:S(2)}) copy-start(f32[512,10]{0,1:T(8,128)S(1)} %get-tuple-element.20) | copy-start | bytes 61444
  850.6 52.6 %copy-start.25 = (f32[512,10]{0,1:T(8,128)}, f32[512,10]{0,1:T(8,128)S(1)}, u32[]{:S(2)}) copy-start(f32[512,10]{0,1:T(8,128)S(1)} %get-tuple-element.45) | copy-start | bytes 61444
  850.6 55.8 %copy-start.20 = (f32[512,10]{0,1:T(8,128)}, f32[512,10]{0,1:T(8,128)S(1)}, u32[]{:S(2)}) copy-start(f32[512,10]{0,1:T(8,128)S(1)} %get-tuple-element.21) | copy-start | bytes 61444
  853.7 11.7 %slice-start.12 = ((s8[10485760]{0:T(1024)(128)(4,1)}), s8[4194304]{0:T(1024)(128)(4,1)S(1)}, s32[]{:S(2)}) async-start(s8[10485760]{0:T(1024)(128)(4,1)} %bitcast.156), calls=%async_computation.20 | async-start | bytes 8388608
  868.6 21.6 %slice-start.9 = ((s8[10485760]{0:T(1024)(128)(4,1)}), s8[4194304]{0:T(1024)(128)(4,1)S(1)}, s32[]{:S(2)}) async-start(s8[10485760]{0:T(1024)(128)(4,1)} %bitcast.154), calls=%async_computation.17 | async-start | bytes 8388608
  868.6 21.6 %slice-start.10 = ((s8[10485760]{0:T(1024)(128)(4,1)}), s8[4194304]{0:T(1024)(128)(4,1)S(1)}, s32[]{:S(2)}) async-start(s8[10485760]{0:T(1024)(128)(4,1)} %bitcast.154), calls=%async_computation.18 | async-start | bytes 8388608
  880.3 22.9 %slice-start.6 = ((s8[10485760]{0:T(1024)(128)(4,1)}), s8[4194304]{0:T(1024)(128)(4,1)S(1)}, s32[]{:S(2)}) async-start(s8[10485760]{0:T(1024)(128)(4,1)} %bitcast.152), calls=%async_computation.14 | async-start | bytes 8388608
  880.3 22.9 %slice-start.7 = ((s8[10485760]{0:T(1024)(128)(4,1)}), s8[4194304]{0:T(1024)(128)(4,1)S(1)}, s32[]{:S(2)}) async-start(s8[10485760]{0:T(1024)(128)(4,1)} %bitcast.152), calls=%async_computation.15 | async-start | bytes 8388608
  893.3 13.2 %slice-start = ((s8[10485760]{0:T(1024)(128)(4,1)}), s8[4194304]{0:T(1024)(128)(4,1)S(1)}, s32[]{:S(2)}) async-start(s8[10485760]{0:T(1024)(128)(4,1)} %bitcast.148), calls=%async_computation.8 | async-start | bytes 8388608
  893.3 13.2 %slice-start.1 = ((s8[10485760]{0:T(1024)(128)(4,1)}), s8[4194304]{0:T(1024)(128)(4,1)S(1)}, s32[]{:S(2)}) async-start(s8[10485760]{0:T(1024)(128)(4,1)} %bitcast.148), calls=%async_computation.9 | async-start | bytes 8388608
  893.3 13.2 %slice-start.2 = ((s8[10485760]{0:T(1024)(128)(4,1)}), s8[2097152]{0:T(1024)(128)(4,1)S(1)}, s32[]{:S(2)}) async-start(s8[10485760]{0:T(1024)(128)(4,1)} %bitcast.148), calls=%async_computation.10 | async-start | bytes 4194304
  909.6 12.1 %copy-start.7 = (bf16[1,2048,256]{1,2,0:T(8,128)(2,1)S(1)}, bf16[1,2048,256]{1,2,0:T(8,128)(2,1)}, u32[]{:S(2)}) copy-start(bf16[1,2048,256]{1,2,0:T(8,128)(2,1)} %all-gather.15.cloned.1.call-done) | copy-start | bytes 3145732
  (24 other events, 185.3 us)
Sparse Core Ops, SparseCore 0:
  17.5 23.2 all-gather.6
  42.5 54.6 all-gather.14
  99.3 684.5 all-gather.10
  794.2 16.8 all-gather.8
  826.8 21.0 all-gather.12
